TPU v7x, 32 devices: a whole 2x2x4 slice. The times are simulated.
32 devices in a mesh: dp: 4 (over x, core), expert: 8 (over z, y).
Axes of the slice: x: 2, y: 2, z: 4, core: 2. Of those that a mesh axis runs over, the one named last changes fastest.
Arguments:
- tokens: bfloat16 [4096, 1024], P(('dp', 'expert')), may hold values from -6 to 6
- expert_ids: int32 [4096, 1], P(('dp', 'expert')), may hold values from 0 to 7; in each aligned block of 128 rows (0 to 127, 128 to 255, ...) at most 48 rows name the same one
- gate_scale: float32 [4096], P(('dp', 'expert')), may hold values from 0.1 to 1
- w_gate_up: bfloat16 [8, 1024, 768], P('expert'), may hold values from -0.1875 to 0.1875
- w_down: bfloat16 [8, 1024, 384], P('expert'), may hold values from -0.3125 to 0.3125
- out_grad: bfloat16 [4096, 1024], P(('dp', 'expert')), may hold values from -1.5 to 1.5
Outputs:
- mixed: bfloat16 [4096, 1024], P(('dp', 'expert'))
- input_rows: bfloat16 [4096, 1024], P(('dp', 'expert'))
- gate_grad_rows: float32 [4096], P(('dp', 'expert'))
- grad_gate_up: float32 [8, 1024, 768], P('expert', 'dp')
- grad_down: float32 [8, 1024, 384], P('expert', 'dp')
Inputs may be any that keep to these rules, and one draw needn't show every extreme that they name: `expert_ids`: among the rows of one device no expert is named more than 48 times, a bound that some block reaches.
All inputs are finite; a program needn't handle non-finite values.
Results may differ from a plain program's by a relative error of at most 0.017.
Values may be sent and summed in bfloat16 or wider, within the bound.
A program may use at most 64 MiB of HBM per device.

v0:
```python
import jax
import jax.numpy as jnp
from jax import lax
from jax.sharding import PartitionSpec as P

BLOCK = 128


def slot_places(route_ids, experts, capacity):
    onehot = (route_ids[:, None] == jnp.arange(experts, dtype=jnp.int32)[None, :]).astype(jnp.int32)
    before = jnp.cumsum(onehot, axis=0) - onehot
    position = jnp.sum(before * onehot, axis=1)
    slot_index = route_ids * capacity + position
    return (slot_index[None, :] == jnp.arange(experts * capacity, dtype=jnp.int32)[:, None]).astype(
        jnp.bfloat16
    )


def contract_rows(left, right):
    return lax.dot_general(
        left, right, (((0,), (0,)), ((), ())), preferred_element_type=jnp.float32
    )


def contract_last(left, right):
    return lax.dot_general(
        left, right, (((1,), (1,)), ((), ())), preferred_element_type=jnp.float32
    )


def expert_forward(slot_rows, weight_in, weight_out):
    hidden_units = weight_out.shape[1]
    gate_up = jnp.dot(slot_rows, weight_in, preferred_element_type=jnp.float32)
    gate_part = gate_up[:, :hidden_units]
    up_part = gate_up[:, hidden_units:]
    hidden = (gate_part * jax.nn.sigmoid(gate_part) * up_part).astype(jnp.bfloat16)
    result = contract_last(hidden, weight_out).astype(jnp.bfloat16)
    return (gate_part, up_part, hidden, result)


def expert_backward(slot_grads, gate_part, up_part, weight_in, weight_out):
    hidden_grad = jnp.dot(slot_grads, weight_out, preferred_element_type=jnp.float32)
    sig_gate = jax.nn.sigmoid(gate_part)
    gate_grad = hidden_grad * up_part * sig_gate * (1.0 + gate_part * (1.0 - sig_gate))
    up_grad = hidden_grad * gate_part * sig_gate
    both_grads = jnp.concatenate([gate_grad, up_grad], axis=1).astype(jnp.bfloat16)
    input_grad = contract_last(both_grads, weight_in).astype(jnp.bfloat16)
    return (both_grads, input_grad)


def pick_entry(table, wanted):
    entries = table.shape[-1]
    chosen = (jnp.arange(entries, dtype=jnp.int32) == wanted).astype(jnp.int32)
    return jnp.sum(table * chosen, axis=-1)


def run_blocks(block_source, grad_source, live_rows, weight_in, weight_out):
    length, model_width = block_source.shape
    hidden_units = weight_out.shape[1]
    start_buffers = (
        jnp.zeros((length, model_width), jnp.bfloat16),
        jnp.zeros((length, model_width), jnp.bfloat16),
        jnp.zeros((length, 2 * hidden_units), jnp.bfloat16),
        jnp.zeros((length, hidden_units), jnp.bfloat16),
    )

    def one_block(block_index, buffers):
        first_row = block_index * BLOCK
        block_rows = lax.dynamic_slice_in_dim(block_source, first_row, BLOCK, 0)
        block_grads = lax.dynamic_slice_in_dim(grad_source, first_row, BLOCK, 0)
        gate_part, up_part, hidden, result = expert_forward(block_rows, weight_in, weight_out)
        both_grads, input_grad = expert_backward(
            block_grads, gate_part, up_part, weight_in, weight_out
        )
        fresh = (result, input_grad, both_grads, hidden)
        return tuple(
            (
                lax.dynamic_update_slice_in_dim(buffer, update, first_row, 0)
                for buffer, update in zip(buffers, fresh)
            )
        )

    block_count = (live_rows + BLOCK - 1) // BLOCK
    return lax.fori_loop(0, block_count, one_block, start_buffers)


def on_device(tokens, expert_ids, gate_scale, w_gate_up, w_down, out_grad):
    row_count, model_width = tokens.shape
    experts = lax.axis_size("expert")
    capacity = 3 * row_count // experts
    slot_count = experts * capacity
    spare_rows = slot_count // 4
    length = slot_count + spare_rows + BLOCK
    route = expert_ids[:, 0]
    expert_range = jnp.arange(experts, dtype=jnp.int32)
    counts = jnp.sum((route[:, None] == expert_range[None, :]).astype(jnp.int32), axis=0)
    count_table = lax.all_gather(counts[None, :], "expert", axis=0, tiled=True)
    home = lax.axis_index("expert")
    my_counts = pick_entry(count_table, home)
    loads = jnp.sum(count_table, axis=0)
    my_load = pick_entry(loads, home)
    places = slot_places(route, experts, capacity)
    scaled = (gate_scale[:, None] * out_grad.astype(jnp.float32)).astype(jnp.bfloat16)
    send_rows = jnp.dot(places, tokens, preferred_element_type=jnp.float32).astype(jnp.bfloat16)
    send_grads = jnp.dot(places, scaled, preferred_element_type=jnp.float32).astype(jnp.bfloat16)
    slot_rows, slot_grads = (
        lax.all_to_all(send_rows, "expert", split_axis=0, concat_axis=0, tiled=True),
        lax.all_to_all(send_grads, "expert", split_axis=0, concat_axis=0, tiled=True),
    )
    starts = jnp.cumsum(my_counts) - my_counts
    ends = starts + my_counts
    position = jnp.arange(length, dtype=jnp.int32)
    sender = jnp.sum((ends[None, :] <= position[:, None]).astype(jnp.int32), axis=1)
    sender = jnp.minimum(sender, experts - 1)
    live = position < my_load
    source = jnp.where(
        live, sender * capacity + position - pick_entry(starts[None, :], sender[:, None]), 0
    )
    compact_rows = jnp.where(
        live[:, None], jnp.take(slot_rows, source, axis=0), jnp.zeros((), jnp.bfloat16)
    )
    compact_grads = jnp.where(
        live[:, None], jnp.take(slot_grads, source, axis=0), jnp.zeros((), jnp.bfloat16)
    )
    weight_in = w_gate_up[0]
    weight_out = w_down[0]
    buffers = run_blocks(compact_rows, compact_grads, my_load, weight_in, weight_out)
    result_buffer, ingrad_buffer, both_buffer, hidden_buffer = buffers
    term_width = both_buffer.shape[1] + hidden_buffer.shape[1]
    all_blocks = (my_load + BLOCK - 1) // BLOCK
    slot_index = jnp.arange(slot_count, dtype=jnp.int32)
    slot_sender = slot_index // capacity
    slot_rank = slot_index % capacity
    slot_live = slot_rank < pick_entry(my_counts[None, :], slot_sender[:, None])
    slot_source = jnp.where(
        slot_live, pick_entry(starts[None, :], slot_sender[:, None]) + slot_rank, 0
    )
    back_result = jnp.where(
        slot_live[:, None],
        jnp.take(result_buffer, slot_source, axis=0),
        jnp.zeros((), jnp.bfloat16),
    )
    back_ingrad = jnp.where(
        slot_live[:, None],
        jnp.take(ingrad_buffer, slot_source, axis=0),
        jnp.zeros((), jnp.bfloat16),
    )
    got_result, got_ingrad = (
        lax.all_to_all(back_result, "expert", split_axis=0, concat_axis=0, tiled=True),
        lax.all_to_all(back_ingrad, "expert", split_axis=0, concat_axis=0, tiled=True),
    )

    def add_block(block_index, running):
        first_row = block_index * BLOCK
        rows_part = lax.dynamic_slice(compact_rows, (first_row, 0), (BLOCK, model_width))
        grads_part = lax.dynamic_slice(compact_grads, (first_row, 0), (BLOCK, model_width))
        both_part = lax.dynamic_slice_in_dim(both_buffer, first_row, BLOCK, 0)
        hidden_part = lax.dynamic_slice_in_dim(hidden_buffer, first_row, BLOCK, 0)
        return running + jnp.concatenate(
            [contract_rows(rows_part, both_part), contract_rows(grads_part, hidden_part)], axis=1
        )

    summed = lax.psum_scatter(
        lax.fori_loop(
            0, all_blocks, add_block, jnp.zeros((model_width, term_width), jnp.float32)
        ).astype(jnp.bfloat16),
        "dp",
        scatter_dimension=0,
        tiled=True,
    ).astype(jnp.float32)
    pair_width = weight_in.shape[1]
    ffn_rows = contract_rows(places, got_result)
    mixed = (gate_scale[:, None] * ffn_rows).astype(jnp.bfloat16)
    gate_grad_rows = jnp.sum(out_grad.astype(jnp.float32) * ffn_rows, axis=1)
    input_rows = contract_rows(places, got_ingrad).astype(jnp.bfloat16)
    return (
        mixed,
        input_rows,
        gate_grad_rows,
        summed[:, :pair_width][None],
        summed[:, pair_width:][None],
    )


def solution(mesh):
    return jax.shard_map(
        on_device,
        mesh=mesh,
        in_specs=(
            P(("dp", "expert"), None),
            P(("dp", "expert"), None),
            P(("dp", "expert")),
            P("expert", None, None),
            P("expert", None, None),
            P(("dp", "expert"), None),
        ),
        out_specs=(
            P(("dp", "expert"), None),
            P(("dp", "expert"), None),
            P(("dp", "expert")),
            P("expert", "dp", None),
            P("expert", "dp", None),
        ),
        check_vma=False,
    )
```

profile of v0, /device:TPU:0, one launch (start us, length us, event | category | flops | bytes accessed | tf_op | source)
XLA Modules:
  0.0 183.9 jit_solution(4433873864724181451)
XLA Ops:
  7.2 0.0 copy-start
  7.2 0.8 fusion.27
  8.0 0.2 reduce_window_sum.18
  8.1 0.8 select_reduce_fusion
  9.0 0.7 multiply_add_fusion
  9.6 2.3 %convolution_convert_fusion.2 = bf16[384,1024]{1,0:T(8,128)(2,1)} fusion(bf16[128,1024]{1,0:T(8,128)(2,1)} %param.19, f32[128]{0:T(128)} %param.16, s32[128]{0:T(128)S(1)} %multiply_add_fusion), kind=kOutput, calls=%fused_computation.31 | convolution fusion | flops 101498880 | bytes 1049600 | tf_op jit(solution)/shard_map/dot_general | solution.py:105
  11.9 7.3 %all-to-all-start.1 = ((bf16[8,48,1024]{2,1,0:T(8,128)(2,1)}), bf16[8,48,1024]{2,1,0:T(8,128)(2,1)S(1)}, u32[]{:S(2)}, u32[]{:S(2)}) async-start(bf16[8,48,1024]{2,1,0:T(8,128)(2,1)} %bitcast.8), calls=%async_computation.1 | async-start | bytes 1572864 | tf_op jit(solution)/shard_map/all_to_all | solution.py:108
  19.2 0.0 copy-done
  19.2 0.0 copy-start.11
  19.2 1.2 convolution_convert_fusion.3
  20.5 18.9 %all-to-all-done.1 = bf16[8,48,1024]{2,1,0:T(8,128)(2,1)S(1)} async-done(((bf16[8,48,1024]{2,1,0:T(8,128)(2,1)}), bf16[8,48,1024]{2,1,0:T(8,128)(2,1)S(1)}, u32[]{:S(2)}, u32[]{:S(2)}) %all-to-all-start.1) | async-done | bytes 786464 | tf_op jit(solution)/shard_map/all_to_all | solution.py:108
  39.4 3.6 %all-to-all-start = ((bf16[8,48,1024]{2,1,0:T(8,128)(2,1)}), bf16[8,48,1024]{2,1,0:T(8,128)(2,1)S(1)}, u32[]{:S(2)}, u32[]{:S(2)}) async-start(bf16[8,48,1024]{2,1,0:T(8,128)(2,1)} %bitcast.4), calls=%async_computation | async-start | bytes 1572864 | tf_op jit(solution)/shard_map/all_to_all | solution.py:107
  43.0 0.0 reduce-scatter.2.cloned.1.call-start
  43.0 0.6 dynamic-slice
  44.3 0.2 dynamic-update-slice
  44.5 19.0 %all-reduce = s32[64]{0:T(128)S(1)} all-reduce(s32[64]{0:T(128)S(1)} %dynamic-update-slice), channel_id=2, replica_groups=mesh['dp'=4,'expert'=8] {'expert'}, use_global_device_ids=true, to_apply=%add | all-reduce | flops 64 | bytes 512
  63.5 0.1 reshape.132
  63.6 0.1 multiply_reduce_fusion
  63.7 0.6 fusion.35
  65.0 0.2 reduce-window.7
  65.2 0.1 convert_reduce_fusion
  65.3 0.1 select_reduce_fusion.1
  65.4 0.7 compare_and_fusion
  66.1 2.9 %gather_fusion.1 = bf16[608,1024]{1,0:T(8,128)(2,1)S(1)} fusion(bf16[384,1024]{1,0:T(8,128)(2,1)S(1)} %bitcast.39, s32[1024]{0:T(1024)S(1)} %pad_clamp_fusion.1), kind=kCustom, calls=%fused_computation.2.clone | custom fusion | bytes 2492800 | tf_op jit(solution)/shard_map/jit(_take)/gather | solution.py:123
  69.0 0.0 all-to-all-done
  69.0 3.5 %gather_fusion = bf16[608,1024]{1,0:T(8,128)(2,1)} fusion(bf16[384,1024]{1,0:T(8,128)(2,1)S(1)} %bitcast.40, s32[1024]{0:T(1024)S(1)} %pad_clamp_fusion.1), kind=kCustom, calls=%fused_computation.clone | custom fusion | bytes 2492800 | tf_op jit(solution)/shard_map/jit(_take)/gather | solution.py:120
  72.5 3.1 %select_select_fusion = (bf16[608,1024]{1,0:T(8,128)(2,1)}, bf16[608,1024]{1,0:T(8,128)(2,1)}) fusion(bf16[608,1024]{1,0:T(8,128)(2,1)S(1)} %gather_fusion.1, pred[608]{0:T(1024)(128)(4,1)S(1)} %get-tuple-element.151, pred[608]{0:T(1024)(128)(4,1)S(1)} %get-tuple-element.161, bf16[608,1024]{1,0:T(8,128)(2,1)} %gather_fusion), kind=kLoop, calls=%fused_computation.33 | loop fusion | flops 2490368 | bytes 4981952 | tf_op jit(solution)/shard_map/jit(_where)/select_n | solution.py:122
  75.6 1.0 broadcast_in_dim.96
  76.6 0.1 broadcast.86.clone
  76.7 1.2 broadcast.86
  77.9 0.4 copy-done.3
  78.3 5.2 %while.26 = (s32[]{:T(128)}, bf16[608,1024]{1,0:T(8,128)(2,1)}, bf16[608,1024]{1,0:T(8,128)(2,1)S(1)}, bf16[608,768]{1,0:T(8,128)(2,1)}, bf16[608,384]{1,0:T(8,1...) while((s32[]{:T(128)}, bf16[608,1024]{1,0:T(8,128)(2,1)}, ...), condition=%wide.region_11.13_spmd, body=%wide.region_10.12_spmd.sunk | while | flops 605962240 | bytes 11174119 | solution.py:84
  78.3 1.4 fusion.67
  79.8 0.0 copy-done.5
  79.8 1.3 multiply_convert_fusion.6
  81.0 0.1 constant_dynamic-update-slice_fusion.2
  81.1 0.7 fusion.70
  81.8 0.6 fusion.69
  82.5 1.1 fusion.68
  83.6 2.7 %broadcast_in_dim.101 = f32[1024,1152]{0,1:T(8,128)} broadcast(f32[]{:T(128)} %constant.102.clone.1), dimensions={} | broadcast | bytes 4718596 | tf_op jit(solution)/shard_map/broadcast_in_dim | solution.py:165
  86.3 7.0 %while.27 = (s32[]{:T(128)}, f32[1024,1152]{0,1:T(8,128)}, s32[]{:T(128)}, bf16[608,1024]{1,0:T(8,128)(2,1)}, bf16[608,768]{1,0:T(8,128)(2,1)}, /*index=5*/bf16[...) while((s32[]{:T(128)}, f32[1024,1152]{0,1:T(8,128)}, ...), condition=%wide.region_15.18_spmd, body=%wide.region_14.17_spmd.sunk | while | flops 304349184 | bytes 57444560 | solution.py:164
  86.3 1.5 fusion.75
  87.8 1.6 fusion.76
  89.4 0.0 copy-done.1
  89.5 1.7 maximum_add_fusion.2
  91.2 2.1 %copy-done.2 = f32[1024,1152]{0,1:T(8,128)} copy-done((f32[1024,1152]{0,1:T(8,128)}, f32[1024,1152]{0,1:T(8,128)S(1)}, u32[]{:S(2)}) %copy-start.2) | copy-done | bytes 4718616 | tf_op jit(solution)/shard_map/while
  93.3 4.9 %copy.12 = bf16[1024,1152]{1,0:T(8,128)(2,1)} copy(f32[1024,1152]{0,1:T(8,128)} %get-tuple-element.105) | data formatting | bytes 7077888 | tf_op jit(solution)/shard_map/while | solution.py:164
  98.2 0.0 reduce-scatter.2.cloned.1.call-update
  98.3 0.6 copy-done.10
  98.9 0.1 select_reduce_fusion.2
  99.0 0.5 compare_and_fusion.1
  99.5 0.0 copy-done.4
  99.5 2.1 %gather_fusion.2 = bf16[384,1024]{1,0:T(8,128)(2,1)S(1)} fusion(bf16[608,1024]{1,0:T(8,128)(2,1)S(1)} %copy-done.4, s32[1024]{0:T(1024)S(1)} %pad_clamp_fusion), kind=kCustom, calls=%fused_computation.1.clone | custom fusion | bytes 1574400 | tf_op jit(solution)/shard_map/jit(_take)/gather | solution.py:140
  101.6 0.0 copy-start.8
  101.6 2.1 %gather_fusion.3 = bf16[384,1024]{1,0:T(8,128)(2,1)S(1)} fusion(bf16[608,1024]{1,0:T(8,128)(2,1)S(1)} %get-tuple-element.102, s32[1024]{0:T(1024)S(1)} %pad_clamp_fusion), kind=kCustom, calls=%fused_computation.3.clone | custom fusion | bytes 1574400 | tf_op jit(solution)/shard_map/jit(_take)/gather | solution.py:145
  103.7 1.1 select_select_fusion.2
  104.9 44.0 %all_to_all.48 = bf16[8,48,1024]{2,1,0:T(8,128)(2,1)S(1)} all-to-all(bf16[8,48,1024]{2,1,0:T(8,128)(2,1)S(1)} %bitcast.44), channel_id=1, replica_groups=mesh['dp'=4,'expert'=8] {'expert'}, dimensions={0} | all-to-all | bytes 1572864 | tf_op jit(solution)/shard_map/all_to_all | solution.py:150
  148.9 3.7 %all-to-all-start.2 = ((bf16[8,48,1024]{2,1,0:T(8,128)(2,1)}), bf16[8,48,1024]{2,1,0:T(8,128)(2,1)S(1)}, u32[]{:S(2)}, u32[]{:S(2)}) async-start(bf16[8,48,1024]{2,1,0:T(8,128)(2,1)} %bitcast.10), calls=%async_computation.2 | async-start | bytes 1572864 | tf_op jit(solution)/shard_map/all_to_all | solution.py:149
  152.6 1.1 convolution_convert_fusion.4
  153.7 18.8 %all-to-all-done.2 = bf16[8,48,1024]{2,1,0:T(8,128)(2,1)S(1)} async-done(((bf16[8,48,1024]{2,1,0:T(8,128)(2,1)}), bf16[8,48,1024]{2,1,0:T(8,128)(2,1)S(1)}, u32[]{:S(2)}, u32[]{:S(2)}) %all-to-all-start.2) | async-done | bytes 786464 | tf_op jit(solution)/shard_map/all_to_all | solution.py:149
  172.5 1.7 fusion.19
  174.2 1.1 convert_element_type.64
  175.3 0.8 slice_bitcast_fusion.1
  176.1 0.9 slice_bitcast_fusion
  (23 shorter events, 0.1 us)
Async XLA Ops:
  7.2 12.1 %copy-start = (bf16[128,1024]{1,0:T(8,128)(2,1)S(1)}, bf16[128,1024]{1,0:T(8,128)(2,1)}, u32[]{:S(2)}) copy-start(bf16[128,1024]{1,0:T(8,128)(2,1)} %param.14) | copy-start | bytes 786436
  11.9 27.5 %all-to-all-start.1 = ((bf16[8,48,1024]{2,1,0:T(8,128)(2,1)}), bf16[8,48,1024]{2,1,0:T(8,128)(2,1)S(1)}, u32[]{:S(2)}, u32[]{:S(2)}) async-start(bf16[8,48,1024]{2,1,0:T(8,128)(2,1)} %bitcast.8), calls=%async_computation.1 | async-start | bytes 1572864 | tf_op jit(solution)/shard_map/all_to_all | solution.py:108
  19.2 23.8 %copy-start.11 = (u32[32]{0:T(128)S(1)}, u32[32]{0:T(128)}, u32[]{:S(2)}) copy-start(u32[32]{0:T(128)} %constant.107) | copy-start | bytes 388
  39.4 29.6 %all-to-all-start = ((bf16[8,48,1024]{2,1,0:T(8,128)(2,1)}), bf16[8,48,1024]{2,1,0:T(8,128)(2,1)S(1)}, u32[]{:S(2)}, u32[]{:S(2)}) async-start(bf16[8,48,1024]{2,1,0:T(8,128)(2,1)} %bitcast.4), calls=%async_computation | async-start | bytes 1572864 | tf_op jit(solution)/shard_map/all_to_all | solution.py:107
  43.0 131.2 %reduce-scatter.2.cloned.1.call-start = ((), (), s32[]{:S(2)}) async-start(), calls=%async_computation.5 | async-start | bytes 2949120 | tf_op jit(solution)/shard_map/reduce_scatter | solution.py:163
  63.7 2.4 %copy-start.9 = (s32[8]{0:T(128)}, s32[8]{0:T(128)S(1)}, u32[]{:S(2)}) copy-start(s32[8]{0:T(128)S(1)} %get-tuple-element.106) | copy-start | bytes 100
  76.6 1.8 copy-start.3
  78.3 1.4 copy-start.5
  86.3 3.1 %copy-start.1 = (f32[1024,1152]{0,1:T(8,128)S(1)}, f32[1024,1152]{0,1:T(8,128)}, u32[]{:S(2)}) copy-start(f32[1024,1152]{0,1:T(8,128)} %get-tuple-element.330) | copy-start | bytes 14155780 | tf_op jit(solution)/shard_map/while
  91.2 2.1 %copy-start.2 = (f32[1024,1152]{0,1:T(8,128)}, f32[1024,1152]{0,1:T(8,128)S(1)}, u32[]{:S(2)}) copy-start(f32[1024,1152]{0,1:T(8,128)S(1)} %maximum_add_fusion.2) | copy-start | bytes 14155780 | tf_op jit(solution)/shard_map/while
  98.2 0.7 copy-start.10
  98.2 1.3 copy-start.4
  101.6 2.1 %copy-start.8 = (pred[384]{0:T(512)(128)(4,1)S(1)}, pred[384]{0:T(512)(128)(4,1)}, u32[]{:S(2)}) copy-start(pred[384]{0:T(512)(128)(4,1)} %get-tuple-element.150) | copy-start | bytes 1156
  148.9 23.7 %copy-start.6 = (bf16[128,1024]{1,0:T(8,128)(2,1)S(1)}, bf16[128,1024]{1,0:T(8,128)(2,1)}, u32[]{:S(2)}) copy-start(bf16[128,1024]{1,0:T(8,128)(2,1)} %param.19) | copy-start | bytes 786436
  148.9 23.7 %copy-start.7 = (f32[128]{0:T(128)S(1)}, f32[128]{0:T(128)}, u32[]{:S(2)}) copy-start(f32[128]{0:T(128)} %param.16) | copy-start | bytes 1540
  148.9 23.7 %all-to-all-start.2 = ((bf16[8,48,1024]{2,1,0:T(8,128)(2,1)}), bf16[8,48,1024]{2,1,0:T(8,128)(2,1)S(1)}, u32[]{:S(2)}, u32[]{:S(2)}) async-start(bf16[8,48,1024]{2,1,0:T(8,128)(2,1)} %bitcast.10), calls=%async_computation.2 | async-start | bytes 1572864 | tf_op jit(solution)/shard_map/all_to_all | solution.py:149
Sparse Core Ops, SparseCore 0:
  98.4 52.2 reduce-scatter.1
where the time goes:
time: 185 us; the launch traced here: 184 us
  blocking collectives  63 us (34%)
  waiting for transfers between devices  37.8 us (20%)
  local copies, waits for them, and re-layouts  26.4 us (14%)
  between operations  15.5 us (8%)
  starting transfers between devices  14.7 us (8%)
  matrix products  13.8 us (7%)
  other arithmetic  12.7 us (7%)
    all_to_all x1, blocking collectives, on_device(): lax.all_to_all(back_ingrad, 'expert', split_axis=0, concat_axis=0, tiled=...  44 us
    unnamed x1, blocking collectives  19 us
    all_to_all x1, waiting for transfers between devices, on_device(): lax.all_to_all(send_grads, 'expert', split_axis=0, concat_axis=0, tiled=T...  18.9 us
    all_to_all x1, waiting for transfers between devices, on_device(): lax.all_to_all(back_result, 'expert', split_axis=0, concat_axis=0, tiled=...  18.8 us
    all_to_all x1, starting transfers between devices, on_device(): lax.all_to_all(send_grads, 'expert', split_axis=0, concat_axis=0, tiled=T...  7.31 us
    dot_general x4, matrix products, contract_rows(): lax.dot_general(left, right, (((0,), (0,)), ((), ())), preferred_element_...  5.85 us
    while x1, local copies, waits for them, and re-layouts, on_device(): lax.fori_loop(0, all_blocks, add_block, jnp.zeros((model_width, term_widt...  4.93 us
    all_to_all x1, starting transfers between devices, on_device(): lax.all_to_all(back_result, 'expert', split_axis=0, concat_axis=0, tiled=...  3.74 us
  transfers between devices with their start and end apart: 4, of which 2 were waited for; matrix products, arithmetic and copies ran while one was open for 8% of the time, Pallas kernels for 0%

commit v1 on v0

--- a/solution.py
+++ b/solution.py
@@ -4,6 +4,30 @@
 from jax.sharding import PartitionSpec as P
 
 BLOCK = 128
+
+
+def cut_along(x, dim, peers):
+    lengths = x.shape
+    blocks = x.reshape(*lengths[:dim], peers, lengths[dim] // peers, *lengths[dim + 1 :])
+    return jnp.moveaxis(blocks, dim, 0)
+
+
+def laid_out(blocks, dim):
+    blocks = jnp.moveaxis(blocks, 0, dim)
+    shape = blocks.shape
+    return blocks.reshape(*shape[:dim], shape[dim] * shape[dim + 1], *shape[dim + 2 :])
+
+
+def exchange_directly(x, axis, split_dim, concat_dim):
+    size, index = (lax.axis_size(axis), lax.axis_index(axis))
+    blocks = cut_along(x, split_dim, size)
+    out = blocks
+    for step in range(1, size):
+        target, source = ((index + step) % size, (index - step) % size)
+        sent = lax.dynamic_index_in_dim(blocks, target, 0)
+        other = lax.ppermute(sent, axis, [(i, (i + step) % size) for i in range(size)])
+        out = lax.dynamic_update_slice_in_dim(out, other, source, axis=0)
+    return laid_out(out, concat_dim)
 
 
 def slot_places(route_ids, experts, capacity):
@@ -105,7 +129,7 @@
     send_grads = jnp.dot(places, scaled, preferred_element_type=jnp.float32).astype(jnp.bfloat16)
     slot_rows, slot_grads = (
         lax.all_to_all(send_rows, "expert", split_axis=0, concat_axis=0, tiled=True),
-        lax.all_to_all(send_grads, "expert", split_axis=0, concat_axis=0, tiled=True),
+        exchange_directly(send_grads, "expert", 0, 0),
     )
     starts = jnp.cumsum(my_counts) - my_counts
     ends = starts + my_counts

time: 185 us -> 187 us (1.011)
  waiting for transfers between devices: 37.8 us -> 29.3 us
  starting transfers between devices: 14.7 us -> 20 us
  blocking collectives: 63 us -> 66.6 us
  local copies, waits for them, and re-layouts: 26.4 us -> 28.4 us
    all_to_all x1 -> x0, waiting for transfers between devices: 18.9 us -> none  [on_device(): lax.all_to_all(send_grads, 'expert', split_axis=0, concat_axis=0, tiled=T...]
    ppermute x0 -> x7, starting transfers between devices: none -> 11.4 us  [exchange_directly(): lax.ppermute(sent, axis, [(i, (i + step) % size) for i in range(size)])]
    ppermute x0 -> x7, waiting for transfers between devices: none -> 10.4 us  [exchange_directly(): lax.ppermute(sent, axis, [(i, (i + step) % size) for i in range(size)])]
    all_to_all x1 -> x0, starting transfers between devices: 7.31 us -> none  [on_device(): lax.all_to_all(send_grads, 'expert', split_axis=0, concat_axis=0, tiled=T...]
    all_to_all x1, blocking collectives: 44 us -> 48.2 us  [on_device(): lax.all_to_all(back_ingrad, 'expert', split_axis=0, concat_axis=0, tiled=...]
  transfers between devices with their start and end apart: 4 -> 10, of which waited for: 2 -> 3; matrix products, arithmetic and copies ran while one was open for 8% -> 9% of each run, Pallas kernels for 0% -> 0%
where the time goes in v1:
time: 187 us
  blocking collectives  66.6 us (36%)
  waiting for transfers between devices  29.3 us (16%)
  local copies, waits for them, and re-layouts  28.4 us (15%)
  starting transfers between devices  20 us (11%)
  between operations  16 us (9%)
  other arithmetic  13.5 us (7%)
  matrix products  12.9 us (7%)
    all_to_all x1, blocking collectives, on_device(): lax.all_to_all(back_ingrad, 'expert', split_axis=0, concat_axis=0, tiled=...  48.2 us
    all_to_all x1, waiting for transfers between devices, on_device(): lax.all_to_all(back_result, 'expert', split_axis=0, concat_axis=0, tiled=...  18.9 us
    unnamed x1, blocking collectives  18.3 us
    ppermute x7, starting transfers between devices, exchange_directly(): lax.ppermute(sent, axis, [(i, (i + step) % size) for i in range(size)])  11.4 us
    ppermute x7, waiting for transfers between devices, exchange_directly(): lax.ppermute(sent, axis, [(i, (i + step) % size) for i in range(size)])  10.4 us
    dot_general x4, matrix products, contract_rows(): lax.dot_general(left, right, (((0,), (0,)), ((), ())), preferred_element_...  5.87 us
    while x1, local copies, waits for them, and re-layouts, on_device(): lax.fori_loop(0, all_blocks, add_block, jnp.zeros((model_width, term_widt...  4.93 us
    all_to_all x1, starting transfers between devices, on_device(): lax.all_to_all(send_rows, 'expert', split_axis=0, concat_axis=0, tiled=True)  4.88 us
  transfers between devices with their start and end apart: 10, of which 3 were waited for; matrix products, arithmetic and copies ran while one was open for 9% of the time, Pallas kernels for 0%

profile of v1, /device:TPU:0, one launch (start us, length us, event | category | flops | bytes accessed | tf_op | source)
XLA Modules:
  0.0 186.6 jit_solution(15124972877308181577)
XLA Ops:
  7.2 0.0 copy-start
  7.2 0.8 fusion.27
  8.0 0.2 reduce_window_sum.18
  8.2 0.8 select_reduce_fusion
  9.0 0.7 multiply_add_fusion
  9.7 1.4 convolution_convert_fusion.2
  11.1 0.0 copy-start.9
  11.1 3.0 %collective-permute-start = (bf16[1,48,1024]{2,1,0:T(8,128)(2,1)S(1)}, bf16[1,48,1024]{2,1,0:T(8,128)(2,1)S(1)}, u32[]{:S(2)}, u32[]{:S(2)}) collective-permute-start(bf16[1,48,1024]{2,1,0:T(8,128)(2,1)S(1)} %constant_dynamic-slice_fusion.6), channel_id=1, source_target_pairs={{0,1},{1,2},{2,3},{3,4},{4,5},{5,6},{6,7},{7,0},{8,9},{9,10},{10,1... | collective-permute-start | bytes 294920 | tf_op jit(solution)/shard_map/ppermute | solution.py:28
  14.1 1.2 convolution_convert_fusion.3
  15.4 4.9 %all-to-all-start = ((bf16[8,48,1024]{2,1,0:T(8,128)(2,1)}), bf16[8,48,1024]{2,1,0:T(8,128)(2,1)S(1)}, u32[]{:S(2)}, u32[]{:S(2)}) async-start(bf16[8,48,1024]{2,1,0:T(8,128)(2,1)} %bitcast.4), calls=%async_computation | async-start | bytes 1572864 | tf_op jit(solution)/shard_map/all_to_all | solution.py:131
  20.3 0.0 reduce-scatter.2.cloned.1.call-start
  20.6 0.6 dynamic-slice
  21.8 0.2 dynamic-update-slice
  22.1 18.3 %all-reduce = s32[64]{0:T(128)S(1)} all-reduce(s32[64]{0:T(128)S(1)} %dynamic-update-slice), channel_id=2, replica_groups=mesh['dp'=4,'expert'=8] {'expert'}, use_global_device_ids=true, to_apply=%add | all-reduce | flops 64 | bytes 512
  40.4 0.1 reshape.138
  40.5 0.1 multiply_reduce_fusion
  40.6 0.6 fusion.35
  41.9 0.2 reduce-window.7
  42.1 0.1 convert_reduce_fusion
  42.3 0.1 select_reduce_fusion.1
  42.4 0.7 compare_and_fusion
  43.0 0.1 constant_dynamic-slice_fusion
  43.1 0.1 collective-permute-start.1
  43.2 0.7 iota_compare_fusion.9
  43.8 4.6 %collective-permute-start.6 = (bf16[1,48,1024]{2,1,0:T(8,128)(2,1)S(1)}, bf16[1,48,1024]{2,1,0:T(8,128)(2,1)S(1)}, u32[]{:S(2)}, u32[]{:S(2)}) collective-permute-start(bf16[1,48,1024]{2,1,0:T(8,128)(2,1)S(1)} %get-tuple-element.155), channel_id=1, source_target_pairs={{0,7},{1,0},{2,1},{3,2},{4,3},{5,4},{6,5},{7,6},{8,15},{9,8},{10,9... | collective-permute-start | bytes 294920 | tf_op jit(solution)/shard_map/ppermute | solution.py:28
  48.5 3.6 %collective-permute-start.3 = (bf16[1,48,1024]{2,1,0:T(8,128)(2,1)S(1)}, bf16[1,48,1024]{2,1,0:T(8,128)(2,1)S(1)}, u32[]{:S(2)}, u32[]{:S(2)}) collective-permute-start(bf16[1,48,1024]{2,1,0:T(8,128)(2,1)S(1)} %get-tuple-element.158), channel_id=1, source_target_pairs={{0,4},{1,5},{2,6},{3,7},{4,0},{5,1},{6,2},{7,3},{8,12},{9,13},{10,... | collective-permute-start | bytes 294920 | tf_op jit(solution)/shard_map/ppermute | solution.py:28
  52.1 10.1 %collective-permute-done.2 = bf16[1,48,1024]{2,1,0:T(8,128)(2,1)S(1)} collective-permute-done((bf16[1,48,1024]{2,1,0:T(8,128)(2,1)S(1)}, bf16[1,48,1024]{2,1,0:T(8,128)(2,1)S(1)}, u32[]{:S(2)}, u32[]{:S(2)}) %collective-permute-start.2) | collective-permute-done | bytes 98336 | tf_op jit(solution)/shard_map/ppermute | solution.py:28
  62.2 0.2 collective-permute-done.3
  62.6 2.9 %gather_fusion.1 = bf16[608,1024]{1,0:T(8,128)(2,1)S(1)} fusion(bf16[384,1024]{1,0:T(8,128)(2,1)S(1)} %bitcast.40, s32[1024]{0:T(1024)S(1)} %pad_clamp_fusion.1), kind=kCustom, calls=%fused_computation.2.clone | custom fusion | bytes 2492800 | tf_op jit(solution)/shard_map/jit(_take)/gather | solution.py:147
  65.5 3.5 %gather_fusion = bf16[608,1024]{1,0:T(8,128)(2,1)} fusion(bf16[384,1024]{1,0:T(8,128)(2,1)S(1)} %bitcast.42, s32[1024]{0:T(1024)S(1)} %pad_clamp_fusion.1), kind=kCustom, calls=%fused_computation.clone | custom fusion | bytes 2492800 | tf_op jit(solution)/shard_map/jit(_take)/gather | solution.py:144
  69.0 3.1 %select_select_fusion = (bf16[608,1024]{1,0:T(8,128)(2,1)}, bf16[608,1024]{1,0:T(8,128)(2,1)}) fusion(bf16[608,1024]{1,0:T(8,128)(2,1)S(1)} %gather_fusion.1, pred[608]{0:T(1024)(128)(4,1)S(1)} %get-tuple-element.151, pred[608]{0:T(1024)(128)(4,1)S(1)} %iota_compare_fusion.9, bf16[608,1024]{1,0:T(8,128)(2,1)} %gather_fusion), kind=kLoop, calls=%fused_computation.33 | loop fusion | flops 2490368 | bytes 4981952 | tf_op jit(solution)/shard_map/jit(_where)/select_n | solution.py:146
  72.0 0.8 broadcast_in_dim.97
  72.9 1.0 broadcast_in_dim.96
  73.8 0.1 broadcast.100.clone
  74.0 1.2 broadcast.100
  75.2 0.4 copy-done.3
  75.6 5.8 %while.26 = (s32[]{:T(128)}, bf16[608,1024]{1,0:T(8,128)(2,1)}, bf16[608,1024]{1,0:T(8,128)(2,1)S(1)}, bf16[608,768]{1,0:T(8,128)(2,1)}, bf16[608,384]{1,0:T(8,1...) while((s32[]{:T(128)}, bf16[608,1024]{1,0:T(8,128)(2,1)}, ...), condition=%wide.region_11.13_spmd, body=%wide.region_10.12_spmd.sunk | while | flops 605962240 | bytes 11174119 | solution.py:108
  75.6 1.4 fusion.67
  77.0 1.3 multiply_convert_fusion.6
  78.3 0.7 constant_dynamic-update-slice_fusion.9
  79.0 0.7 fusion.70
  79.7 0.6 fusion.69
  80.4 1.1 fusion.68
  81.4 2.7 %broadcast_in_dim.101 = f32[1024,1152]{0,1:T(8,128)} broadcast(f32[]{:T(128)} %constant.205.clone.1), dimensions={} | broadcast | bytes 4718596 | tf_op jit(solution)/shard_map/broadcast_in_dim | solution.py:189
  84.2 7.0 %while.27 = (s32[]{:T(128)}, f32[1024,1152]{0,1:T(8,128)}, s32[]{:T(128)}, bf16[608,1024]{1,0:T(8,128)(2,1)}, bf16[608,768]{1,0:T(8,128)(2,1)}, /*index=5*/bf16[...) while((s32[]{:T(128)}, f32[1024,1152]{0,1:T(8,128)}, ...), condition=%wide.region_15.18_spmd, body=%wide.region_14.17_spmd.sunk | while | flops 304349184 | bytes 57444560 | solution.py:188
  84.2 1.5 fusion.75
  85.7 1.6 fusion.76
  87.4 1.7 maximum_add_fusion.2
  89.1 2.1 %copy-done.2 = f32[1024,1152]{0,1:T(8,128)} copy-done((f32[1024,1152]{0,1:T(8,128)}, f32[1024,1152]{0,1:T(8,128)S(1)}, u32[]{:S(2)}) %copy-start.2) | copy-done | bytes 4718616 | tf_op jit(solution)/shard_map/while
  91.2 4.9 %copy.12 = bf16[1024,1152]{1,0:T(8,128)(2,1)} copy(f32[1024,1152]{0,1:T(8,128)} %get-tuple-element.105) | data formatting | bytes 7077888 | tf_op jit(solution)/shard_map/while | solution.py:188
  96.1 0.0 reduce-scatter.2.cloned.1.call-update
  96.2 0.1 select_reduce_fusion.2
  96.3 1.1 copy-done.4
  97.4 2.7 %gather_fusion.2 = bf16[384,1024]{1,0:T(8,128)(2,1)} fusion(bf16[608,1024]{1,0:T(8,128)(2,1)S(1)} %copy-done.4, s32[1024]{0:T(1024)S(1)} %pad_clamp_fusion), kind=kCustom, calls=%fused_computation.1.clone | custom fusion | bytes 1574400 | tf_op jit(solution)/shard_map/jit(_take)/gather | solution.py:164
  100.1 2.1 %gather_fusion.3 = bf16[384,1024]{1,0:T(8,128)(2,1)S(1)} fusion(bf16[608,1024]{1,0:T(8,128)(2,1)S(1)} %get-tuple-element.102, s32[1024]{0:T(1024)S(1)} %pad_clamp_fusion), kind=kCustom, calls=%fused_computation.3.clone | custom fusion | bytes 1574400 | tf_op jit(solution)/shard_map/jit(_take)/gather | solution.py:169
  102.2 1.1 select_select_fusion.2
  103.3 48.2 %all_to_all.36 = bf16[8,48,1024]{2,1,0:T(8,128)(2,1)S(1)} all-to-all(bf16[8,48,1024]{2,1,0:T(8,128)(2,1)S(1)} %bitcast.46), channel_id=1, replica_groups=mesh['dp'=4,'expert'=8] {'expert'}, dimensions={0} | all-to-all | bytes 1572864 | tf_op jit(solution)/shard_map/all_to_all | solution.py:174
  151.6 3.8 %all-to-all-start.1 = ((bf16[8,48,1024]{2,1,0:T(8,128)(2,1)}), bf16[8,48,1024]{2,1,0:T(8,128)(2,1)S(1)}, u32[]{:S(2)}, u32[]{:S(2)}) async-start(bf16[8,48,1024]{2,1,0:T(8,128)(2,1)} %bitcast.10), calls=%async_computation.1 | async-start | bytes 1572864 | tf_op jit(solution)/shard_map/all_to_all | solution.py:173
  155.3 1.1 convolution_convert_fusion.4
  156.4 18.9 %all-to-all-done.1 = bf16[8,48,1024]{2,1,0:T(8,128)(2,1)S(1)} async-done(((bf16[8,48,1024]{2,1,0:T(8,128)(2,1)}), bf16[8,48,1024]{2,1,0:T(8,128)(2,1)S(1)}, u32[]{:S(2)}, u32[]{:S(2)}) %all-to-all-start.1) | async-done | bytes 786464 | tf_op jit(solution)/shard_map/all_to_all | solution.py:173
  175.3 1.7 fusion.19
  176.9 1.1 convert_element_type.64
  178.1 0.8 slice_bitcast_fusion.1
  178.9 0.9 slice_bitcast_fusion
  (40 shorter events, 0.2 us)
Async XLA Ops:
  7.2 7.0 %copy-start = (bf16[128,1024]{1,0:T(8,128)(2,1)S(1)}, bf16[128,1024]{1,0:T(8,128)(2,1)}, u32[]{:S(2)}) copy-start(bf16[128,1024]{1,0:T(8,128)(2,1)} %param.14) | copy-start | bytes 786436
  11.1 9.5 %copy-start.9 = (u32[32]{0:T(128)S(1)}, u32[32]{0:T(128)}, u32[]{:S(2)}) copy-start(u32[32]{0:T(128)} %constant.210) | copy-start | bytes 388
  11.1 32.0 %collective-permute-start = (bf16[1,48,1024]{2,1,0:T(8,128)(2,1)S(1)}, bf16[1,48,1024]{2,1,0:T(8,128)(2,1)S(1)}, u32[]{:S(2)}, u32[]{:S(2)}) collective-permute-start(bf16[1,48,1024]{2,1,0:T(8,128)(2,1)S(1)} %constant_dynamic-slice_fusion.6), channel_id=1, source_target_pairs={{0,1},{1,2},{2,3},{3,4},{4,5},{5,6},{6,7},{7,0},{8,9},{9,10},{10,1... | collective-permute-start | bytes 294920 | tf_op jit(solution)/shard_map/ppermute | solution.py:28
  15.4 50.1 %all-to-all-start = ((bf16[8,48,1024]{2,1,0:T(8,128)(2,1)}), bf16[8,48,1024]{2,1,0:T(8,128)(2,1)S(1)}, u32[]{:S(2)}, u32[]{:S(2)}) async-start(bf16[8,48,1024]{2,1,0:T(8,128)(2,1)} %bitcast.4), calls=%async_computation | async-start | bytes 1572864 | tf_op jit(solution)/shard_map/all_to_all | solution.py:131
  20.3 156.7 %reduce-scatter.2.cloned.1.call-start = ((), (), s32[]{:S(2)}) async-start(), calls=%async_computation.4 | async-start | bytes 2949120 | tf_op jit(solution)/shard_map/reduce_scatter | solution.py:187
  43.1 9.0 %collective-permute-start.1 = (bf16[1,48,1024]{2,1,0:T(8,128)(2,1)S(1)}, bf16[1,48,1024]{2,1,0:T(8,128)(2,1)S(1)}, u32[]{:S(2)}, u32[]{:S(2)}) collective-permute-start(bf16[1,48,1024]{2,1,0:T(8,128)(2,1)S(1)} %get-tuple-element.160), channel_id=1, source_target_pairs={{0,2},{1,3},{2,4},{3,5},{4,6},{5,7},{6,0},{7,1},{8,10},{9,11},{10,... | collective-permute-start | bytes 294920 | tf_op jit(solution)/shard_map/ppermute | solution.py:28
  43.8 18.7 %collective-permute-start.6 = (bf16[1,48,1024]{2,1,0:T(8,128)(2,1)S(1)}, bf16[1,48,1024]{2,1,0:T(8,128)(2,1)S(1)}, u32[]{:S(2)}, u32[]{:S(2)}) collective-permute-start(bf16[1,48,1024]{2,1,0:T(8,128)(2,1)S(1)} %get-tuple-element.155), channel_id=1, source_target_pairs={{0,7},{1,0},{2,1},{3,2},{4,3},{5,4},{6,5},{7,6},{8,15},{9,8},{10,9... | collective-permute-start | bytes 294920 | tf_op jit(solution)/shard_map/ppermute | solution.py:28
  48.5 14.1 %collective-permute-start.5 = (bf16[1,48,1024]{2,1,0:T(8,128)(2,1)S(1)}, bf16[1,48,1024]{2,1,0:T(8,128)(2,1)S(1)}, u32[]{:S(2)}, u32[]{:S(2)}) collective-permute-start(bf16[1,48,1024]{2,1,0:T(8,128)(2,1)S(1)} %get-tuple-element.156), channel_id=1, source_target_pairs={{0,6},{1,7},{2,0},{3,1},{4,2},{5,3},{6,4},{7,5},{8,14},{9,15},{10,... | collective-permute-start | bytes 294920 | tf_op jit(solution)/shard_map/ppermute | solution.py:28
  48.5 14.0 %collective-permute-start.4 = (bf16[1,48,1024]{2,1,0:T(8,128)(2,1)S(1)}, bf16[1,48,1024]{2,1,0:T(8,128)(2,1)S(1)}, u32[]{:S(2)}, u32[]{:S(2)}) collective-permute-start(bf16[1,48,1024]{2,1,0:T(8,128)(2,1)S(1)} %get-tuple-element.157), channel_id=1, source_target_pairs={{0,5},{1,6},{2,7},{3,0},{4,1},{5,2},{6,3},{7,4},{8,13},{9,14},{10,... | collective-permute-start | bytes 294920 | tf_op jit(solution)/shard_map/ppermute | solution.py:28
  48.5 14.0 %collective-permute-start.3 = (bf16[1,48,1024]{2,1,0:T(8,128)(2,1)S(1)}, bf16[1,48,1024]{2,1,0:T(8,128)(2,1)S(1)}, u32[]{:S(2)}, u32[]{:S(2)}) collective-permute-start(bf16[1,48,1024]{2,1,0:T(8,128)(2,1)S(1)} %get-tuple-element.158), channel_id=1, source_target_pairs={{0,4},{1,5},{2,6},{3,7},{4,0},{5,1},{6,2},{7,3},{8,12},{9,13},{10,... | collective-permute-start | bytes 294920 | tf_op jit(solution)/shard_map/ppermute | solution.py:28
  52.1 10.1 %collective-permute-start.2 = (bf16[1,48,1024]{2,1,0:T(8,128)(2,1)S(1)}, bf16[1,48,1024]{2,1,0:T(8,128)(2,1)S(1)}, u32[]{:S(2)}, u32[]{:S(2)}) collective-permute-start(bf16[1,48,1024]{2,1,0:T(8,128)(2,1)S(1)} %get-tuple-element.159), channel_id=1, source_target_pairs={{0,3},{1,4},{2,5},{3,6},{4,7},{5,0},{6,1},{7,2},{8,11},{9,12},{10,... | collective-permute-start | bytes 294920 | tf_op jit(solution)/shard_map/ppermute | solution.py:28
  73.8 1.8 copy-start.3
  75.6 1.4 copy-start.5
  84.2 3.2 %copy-start.1 = (f32[1024,1152]{0,1:T(8,128)S(1)}, f32[1024,1152]{0,1:T(8,128)}, u32[]{:S(2)}) copy-start(f32[1024,1152]{0,1:T(8,128)} %get-tuple-element.336) | copy-start | bytes 14155780 | tf_op jit(solution)/shard_map/while
  89.0 2.1 %copy-start.2 = (f32[1024,1152]{0,1:T(8,128)}, f32[1024,1152]{0,1:T(8,128)S(1)}, u32[]{:S(2)}) copy-start(f32[1024,1152]{0,1:T(8,128)S(1)} %maximum_add_fusion.2) | copy-start | bytes 14155780 | tf_op jit(solution)/shard_map/while
  96.1 1.3 copy-start.4
  100.1 2.1 %copy-start.6 = (bf16[384,1024]{1,0:T(8,128)(2,1)S(1)}, bf16[384,1024]{1,0:T(8,128)(2,1)}, u32[]{:S(2)}) copy-start(bf16[384,1024]{1,0:T(8,128)(2,1)} %gather_fusion.2) | copy-start | bytes 2359300
  151.6 23.7 %copy-start.7 = (bf16[128,1024]{1,0:T(8,128)(2,1)S(1)}, bf16[128,1024]{1,0:T(8,128)(2,1)}, u32[]{:S(2)}) copy-start(bf16[128,1024]{1,0:T(8,128)(2,1)} %param.19) | copy-start | bytes 786436
  151.6 23.7 %copy-start.8 = (f32[128]{0:T(128)S(1)}, f32[128]{0:T(128)}, u32[]{:S(2)}) copy-start(f32[128]{0:T(128)} %param.16) | copy-start | bytes 1540
  151.6 23.7 %all-to-all-start.1 = ((bf16[8,48,1024]{2,1,0:T(8,128)(2,1)}), bf16[8,48,1024]{2,1,0:T(8,128)(2,1)S(1)}, u32[]{:S(2)}, u32[]{:S(2)}) async-start(bf16[8,48,1024]{2,1,0:T(8,128)(2,1)} %bitcast.10), calls=%async_computation.1 | async-start | bytes 1572864 | tf_op jit(solution)/shard_map/all_to_all | solution.py:173
Sparse Core Ops, SparseCore 0:
  96.3 56.3 reduce-scatter.1
